TPU v7x, 32 devices: a whole 2x2x4 slice. The times are simulated.
32 devices in a mesh: chan: 8 (over z, core), tm: 4 (over y, x).
Axes of the slice: x: 2, y: 2, z: 4, core: 2. Of those that a mesh axis runs over, the one named last changes fastest.
Arguments:
- spectra: bfloat16 [4, 1024, 1024], P('tm', 'chan')
- tile_bin: int32 [32], P('chan'), may hold values from 0 to 7
- owner_bins: int32 [8], replicated, may hold values from 0 to 7, each once
- source_slab: int32 [1], replicated, may hold values from 0 to 255
Outputs:
- stacks: float32 [8, 128, 512], P('chan', 'tm')
Inputs may be any that keep to these rules, and one draw needn't show every extreme that they name: `tile_bin`: a tile of 128 pairs belongs to exactly one offset bin. `owner_bins`: every bin stands once. `source_slab`: the slab's 4 channels lie within one chan index's block.
All inputs are finite; a program needn't handle non-finite values.
Results may differ from a plain program's by a relative error of at most 0.005.
Values may be sent and summed in bfloat16 or wider, within the bound.
A program may use at most 64 MiB of HBM per device.

v0:
```python
import math
import jax
import jax.numpy as jnp
from jax import lax
from jax.sharding import PartitionSpec as P

LAGS = 512
SEG_LEN = 15000
K0 = 60
GROUP = 64
SRC = 4
PAIRS = 128


def shifted(block, axis, distance):
    devices = range(lax.axis_size(axis))
    route = [((i - distance) % len(devices), i) for i in devices]
    return lax.ppermute(block, axis, route)


def whiten_block(raw_block):
    values = raw_block.astype(jnp.float32)
    channels = values.shape[0]
    bands = values.shape[1] // 2
    grouped = values.reshape(channels, 2, bands // GROUP, GROUP)
    power = jnp.mean(grouped[:, 0] * grouped[:, 0] + grouped[:, 1] * grouped[:, 1], axis=-1)
    inverse = 1.0 / jnp.sqrt(power + 1e-06)
    return (grouped * inverse[:, None, :, None]).reshape(channels, 2 * bands).astype(jnp.bfloat16)


def phase_tables(bands, lag_count):
    freq_index = K0 + jnp.arange(bands)
    lag_index = jnp.arange(lag_count) - lag_count // 2
    phase = freq_index[:, None] * lag_index[None, :] % SEG_LEN
    angle = phase.astype(jnp.float32) * (2.0 * math.pi / SEG_LEN)
    return (jnp.cos(angle), jnp.sin(angle))


def modulate(slab_rows, cosines, sines):
    values = slab_rows.astype(jnp.float32)
    bands = cosines.shape[0]
    real_part = values[:, :bands, None]
    imag_part = values[:, bands:, None]
    upper = real_part * cosines[None] + imag_part * sines[None]
    lower = imag_part * cosines[None] - real_part * sines[None]
    return jnp.concatenate([upper, lower], axis=1).astype(jnp.bfloat16)


def normalize(correlation):
    energy = jnp.mean(correlation * correlation, axis=-1, keepdims=True)
    return correlation / jnp.sqrt(energy + 1e-06)


def per_device(spectra, tile_bin, owner_bins, source_slab):
    whitened = whiten_block(spectra[0])
    channels = whitened.shape[0]
    bands = whitened.shape[1] // 2
    cycle_size = lax.axis_size("chan")
    my_index = lax.axis_index("chan")
    slabs_per_block = channels // SRC
    slab_number = source_slab[0]
    root_index = slab_number // slabs_per_block
    own_slab = lax.dynamic_slice_in_dim(whitened, slab_number % slabs_per_block * SRC, SRC, 0)
    initial = jnp.where(my_index == root_index, own_slab, jnp.zeros_like(own_slab))

    def paired_hop(hop_count, state):
        ahead, behind, received = state
        ahead = shifted(ahead, "chan", 1)
        behind = shifted(behind, "chan", -1)
        received = jnp.where((my_index - hop_count) % cycle_size == root_index, ahead, received)
        received = jnp.where((my_index + hop_count) % cycle_size == root_index, behind, received)
        return (ahead, behind, received)

    source_rows = lax.fori_loop(1, cycle_size // 2 + 1, paired_hop, (own_slab, own_slab, initial))[
        2
    ]
    cosines, sines = phase_tables(bands, LAGS)
    modulated = modulate(source_rows, cosines, sines)
    correlation = jnp.einsum("ck,ikl->icl", whitened, modulated, preferred_element_type=jnp.float32)
    traces = normalize(correlation)
    summed = lax.psum(traces, "tm")
    row_count = PAIRS // lax.axis_size("tm")
    own_rows = lax.dynamic_slice_in_dim(summed, lax.axis_index("tm") * row_count, row_count, 1)
    membership = (owner_bins[:, None] == tile_bin[None, :]).astype(jnp.float32)
    stacked = lax.psum_scatter(
        jnp.einsum("rt,tpl->rpl", membership, own_rows, precision=lax.Precision.HIGHEST),
        "chan",
        scatter_dimension=0,
        tiled=True,
    )
    return stacked / lax.axis_size("tm")


def solution(mesh):
    return jax.shard_map(
        per_device,
        mesh=mesh,
        in_specs=(P("tm", "chan", None), P("chan"), P(), P()),
        out_specs=P("chan", "tm", None),
        check_vma=False,
    )
```

profile of v0, /device:TPU:0, one launch (start us, length us, event | category | flops | bytes accessed | tf_op | source)
XLA Modules:
  0.0 135.3 jit_solution(4743199806616281129)
XLA Ops:
  6.5 0.0 all-reduce.2.cloned.1.call-start
  7.3 1.1 copy.14
  8.5 0.1 fusion.11
  8.6 0.1 broadcast_select_fusion
  8.7 0.1 copy.17
  8.9 0.1 copy.15
  9.0 24.5 %while.19 = (s32[]{:T(128)}, bf16[4,1024]{1,0:T(4,128)(2,1)S(1)}, bf16[4,1024]{1,0:T(4,128)(2,1)S(1)}, bf16[4,1024]{1,0:T(4,128)(2,1)S(1)}, s32[]{:T(128)}, /*in...) while((s32[]{:T(128)}, bf16[4,1024]{1,0:T(4,128)(2,1)S(1)}, bf16[4,1024]{1,0:T(4,128)(2,1)S(1)}, ...), condition=%wide.region_2.3_spmd, body=%wide.region_1.2_spmd.sunk | while | flops 8220 | bytes 131515 | solution.py:74
  9.0 4.5 %collective-permute-start.1 = (bf16[4,1024]{1,0:T(4,128)(2,1)S(1)}, bf16[4,1024]{1,0:T(4,128)(2,1)S(1)}, u32[]{:S(2)}, u32[]{:S(2)}) collective-permute-start(bf16[4,1024]{1,0:T(4,128)(2,1)S(1)} %get-tuple-element.246), channel_id=1, source_target_pairs={{4,0},{8,4},{12,8},{16,12},{20,16},{24,20},{28,24},{0,28},{5,1},{9... | collective-permute-start | bytes 24584 | tf_op jit(solution)/shard_map/while/body/eval_jaxpr/ppermute | solution.py:18
  13.6 0.0 collective-permute-start
  13.6 1.4 %collective-permute-done.1 = bf16[4,1024]{1,0:T(4,128)(2,1)S(1)} collective-permute-done((bf16[4,1024]{1,0:T(4,128)(2,1)S(1)}, bf16[4,1024]{1,0:T(4,128)(2,1)S(1)}, u32[]{:S(2)}, u32[]{:S(2)}) %collective-permute-start.1) | collective-permute-done | bytes 8224 | tf_op jit(solution)/shard_map/while/body/eval_jaxpr/ppermute | solution.py:18
  15.0 3.5 %collective-permute-done = bf16[4,1024]{1,0:T(4,128)(2,1)S(1)} collective-permute-done((bf16[4,1024]{1,0:T(4,128)(2,1)S(1)}, bf16[4,1024]{1,0:T(4,128)(2,1)S(1)}, u32[]{:S(2)}, u32[]{:S(2)}) %collective-permute-start) | collective-permute-done | bytes 8224 | tf_op jit(solution)/shard_map/while/body/eval_jaxpr/ppermute | solution.py:18
  18.5 0.1 collective-permute-start.1
  18.6 0.5 collective-permute-start
  19.1 0.9 collective-permute-done.1
  19.9 3.5 %collective-permute-done = bf16[4,1024]{1,0:T(4,128)(2,1)S(1)} collective-permute-done((bf16[4,1024]{1,0:T(4,128)(2,1)S(1)}, bf16[4,1024]{1,0:T(4,128)(2,1)S(1)}, u32[]{:S(2)}, u32[]{:S(2)}) %collective-permute-start) | collective-permute-done | bytes 8224 | tf_op jit(solution)/shard_map/while/body/eval_jaxpr/ppermute | solution.py:18
  23.5 0.1 collective-permute-start.1
  23.6 0.4 collective-permute-start
  24.1 0.9 collective-permute-done.1
  25.0 3.5 %collective-permute-done = bf16[4,1024]{1,0:T(4,128)(2,1)S(1)} collective-permute-done((bf16[4,1024]{1,0:T(4,128)(2,1)S(1)}, bf16[4,1024]{1,0:T(4,128)(2,1)S(1)}, u32[]{:S(2)}, u32[]{:S(2)}) %collective-permute-start) | collective-permute-done | bytes 8224 | tf_op jit(solution)/shard_map/while/body/eval_jaxpr/ppermute | solution.py:18
  28.5 0.1 collective-permute-start.1
  28.6 0.5 collective-permute-start
  29.1 0.9 collective-permute-done.1
  30.0 3.5 %collective-permute-done = bf16[4,1024]{1,0:T(4,128)(2,1)S(1)} collective-permute-done((bf16[4,1024]{1,0:T(4,128)(2,1)S(1)}, bf16[4,1024]{1,0:T(4,128)(2,1)S(1)}, u32[]{:S(2)}, u32[]{:S(2)}) %collective-permute-start) | collective-permute-done | bytes 8224 | tf_op jit(solution)/shard_map/while/body/eval_jaxpr/ppermute | solution.py:18
  33.6 4.3 %fusion.9 = (f32[512,512]{0,1:T(8,128)S(1)}, f32[512,512]{0,1:T(8,128)S(1)}) fusion(s32[512]{0:T(512)S(1)} %get-tuple-element.195, s32[512]{0:T(512)S(1)} %get-tuple-element.196), kind=kLoop, calls=%fused_computation.16 | loop fusion | flops 2359296 | bytes 2101248 | tf_op jit(solution)/shard_map/cos | solution.py:36
  37.9 1.1 add_convert_fusion
  39.0 1.3 multiply_reduce_fusion
  40.3 1.1 divide_bitcast_fusion
  41.4 0.0 copy-start
  41.4 0.0 copy-start.1
  41.4 0.0 all-reduce.2.cloned.1.call-update
  41.4 0.0 reduce-scatter.2.cloned.1.call-start
  41.5 50.9 %all-reduce.2.cloned.1.call-done = f32[4,128,512]{1,2,0:T(8,128)} async-done(((f32[4,128,512]{1,2,0:T(8,128)}), f32[4,128,512]{1,2,0:T(8,128)}) %all-reduce.2.cloned.1.call-update) | async-done | bytes 1048592 | tf_op jit(solution)/shard_map/psum | solution.py:81
  92.3 1.6 %constant_dynamic-slice_fusion = f32[4,32,512]{1,2,0:T(8,128)S(1)} fusion(f32[4,128,512]{1,2,0:T(8,128)} %all-reduce.2.cloned.1.call-done, s32[]{:T(128)S(6)} %select_n.118), kind=kLoop, calls=%fused_computation.36 | loop fusion | bytes 524292 | tf_op jit(solution)/shard_map/dynamic_slice | solution.py:83
  93.9 0.3 copy.19
  94.2 0.0 copy-done
  94.2 0.0 copy-done.1
  94.3 0.5 fusion.15
  94.8 1.1 copy.20
  95.9 0.0 reduce-scatter.2.cloned.1.call-update
  95.9 31.1 %reduce-scatter.2.cloned.1.call-done = f32[1,32,512]{2,1,0:T(8,128)} async-done(((f32[8,32,512]{2,1,0:T(8,128)}), f32[1,32,512]{2,1,0:T(8,128)}) %reduce-scatter.2.cloned.1.call-update) | async-done | bytes 65552 | tf_op jit(solution)/shard_map/reduce_scatter | solution.py:85
  127.0 1.5 %broadcast_multiply_fusion = f32[1,32,512]{2,1,0:T(8,128)} fusion(f32[1,32,512]{2,1,0:T(8,128)} %reduce-scatter.2.cloned.1.call-done), kind=kLoop, calls=%fused_computation.26 | loop fusion | flops 16384 | bytes 131072 | tf_op jit(solution)/shard_map/div | solution.py:91
  (19 shorter events, 0.2 us)
Async XLA Ops:
  6.5 85.8 %all-reduce.2.cloned.1.call-start = ((), (), s32[]{:S(2)}) async-start(), calls=%async_computation.1 | async-start | bytes 2097152 | tf_op jit(solution)/shard_map/psum | solution.py:81
  9.0 5.9 %collective-permute-start.1 = (bf16[4,1024]{1,0:T(4,128)(2,1)S(1)}, bf16[4,1024]{1,0:T(4,128)(2,1)S(1)}, u32[]{:S(2)}, u32[]{:S(2)}) collective-permute-start(bf16[4,1024]{1,0:T(4,128)(2,1)S(1)} %get-tuple-element.246), channel_id=1, source_target_pairs={{4,0},{8,4},{12,8},{16,12},{20,16},{24,20},{28,24},{0,28},{5,1},{9... | collective-permute-start | bytes 24584 | tf_op jit(solution)/shard_map/while/body/eval_jaxpr/ppermute | solution.py:18
  13.6 4.9 %collective-permute-start = (bf16[4,1024]{1,0:T(4,128)(2,1)S(1)}, bf16[4,1024]{1,0:T(4,128)(2,1)S(1)}, u32[]{:S(2)}, u32[]{:S(2)}) collective-permute-start(bf16[4,1024]{1,0:T(4,128)(2,1)S(1)} %get-tuple-element.245), channel_id=1, source_target_pairs={{28,0},{0,4},{4,8},{8,12},{12,16},{16,20},{20,24},{24,28},{29,1},{... | collective-permute-start | bytes 24584 | tf_op jit(solution)/shard_map/while/body/eval_jaxpr/ppermute | solution.py:18
  18.5 1.4 %collective-permute-start.1 = (bf16[4,1024]{1,0:T(4,128)(2,1)S(1)}, bf16[4,1024]{1,0:T(4,128)(2,1)S(1)}, u32[]{:S(2)}, u32[]{:S(2)}) collective-permute-start(bf16[4,1024]{1,0:T(4,128)(2,1)S(1)} %get-tuple-element.246), channel_id=1, source_target_pairs={{4,0},{8,4},{12,8},{16,12},{20,16},{24,20},{28,24},{0,28},{5,1},{9... | collective-permute-start | bytes 24584 | tf_op jit(solution)/shard_map/while/body/eval_jaxpr/ppermute | solution.py:18
  18.6 4.9 %collective-permute-start = (bf16[4,1024]{1,0:T(4,128)(2,1)S(1)}, bf16[4,1024]{1,0:T(4,128)(2,1)S(1)}, u32[]{:S(2)}, u32[]{:S(2)}) collective-permute-start(bf16[4,1024]{1,0:T(4,128)(2,1)S(1)} %get-tuple-element.245), channel_id=1, source_target_pairs={{28,0},{0,4},{4,8},{8,12},{12,16},{16,20},{20,24},{24,28},{29,1},{... | collective-permute-start | bytes 24584 | tf_op jit(solution)/shard_map/while/body/eval_jaxpr/ppermute | solution.py:18
  23.5 1.5 %collective-permute-start.1 = (bf16[4,1024]{1,0:T(4,128)(2,1)S(1)}, bf16[4,1024]{1,0:T(4,128)(2,1)S(1)}, u32[]{:S(2)}, u32[]{:S(2)}) collective-permute-start(bf16[4,1024]{1,0:T(4,128)(2,1)S(1)} %get-tuple-element.246), channel_id=1, source_target_pairs={{4,0},{8,4},{12,8},{16,12},{20,16},{24,20},{28,24},{0,28},{5,1},{9... | collective-permute-start | bytes 24584 | tf_op jit(solution)/shard_map/while/body/eval_jaxpr/ppermute | solution.py:18
  23.6 4.9 %collective-permute-start = (bf16[4,1024]{1,0:T(4,128)(2,1)S(1)}, bf16[4,1024]{1,0:T(4,128)(2,1)S(1)}, u32[]{:S(2)}, u32[]{:S(2)}) collective-permute-start(bf16[4,1024]{1,0:T(4,128)(2,1)S(1)} %get-tuple-element.245), channel_id=1, source_target_pairs={{28,0},{0,4},{4,8},{8,12},{12,16},{16,20},{20,24},{24,28},{29,1},{... | collective-permute-start | bytes 24584 | tf_op jit(solution)/shard_map/while/body/eval_jaxpr/ppermute | solution.py:18
  28.5 1.4 %collective-permute-start.1 = (bf16[4,1024]{1,0:T(4,128)(2,1)S(1)}, bf16[4,1024]{1,0:T(4,128)(2,1)S(1)}, u32[]{:S(2)}, u32[]{:S(2)}) collective-permute-start(bf16[4,1024]{1,0:T(4,128)(2,1)S(1)} %get-tuple-element.246), channel_id=1, source_target_pairs={{4,0},{8,4},{12,8},{16,12},{20,16},{24,20},{28,24},{0,28},{5,1},{9... | collective-permute-start | bytes 24584 | tf_op jit(solution)/shard_map/while/body/eval_jaxpr/ppermute | solution.py:18
  28.6 4.9 %collective-permute-start = (bf16[4,1024]{1,0:T(4,128)(2,1)S(1)}, bf16[4,1024]{1,0:T(4,128)(2,1)S(1)}, u32[]{:S(2)}, u32[]{:S(2)}) collective-permute-start(bf16[4,1024]{1,0:T(4,128)(2,1)S(1)} %get-tuple-element.245), channel_id=1, source_target_pairs={{28,0},{0,4},{4,8},{8,12},{12,16},{16,20},{20,24},{24,28},{29,1},{... | collective-permute-start | bytes 24584 | tf_op jit(solution)/shard_map/while/body/eval_jaxpr/ppermute | solution.py:18
  41.4 52.8 %copy-start = (s32[8]{0:T(128)S(1)}, s32[8]{0:T(128)}, u32[]{:S(2)}) copy-start(s32[8]{0:T(128)} %param.8) | copy-start | bytes 100
  41.4 52.8 %copy-start.1 = (s32[4]{0:T(128)S(1)}, s32[4]{0:T(128)}, u32[]{:S(2)}) copy-start(s32[4]{0:T(128)} %param.7) | copy-start | bytes 52
  41.4 85.5 %reduce-scatter.2.cloned.1.call-start = ((), (), s32[]{:S(2)}) async-start(), calls=%async_computation.2 | async-start | bytes 589824 | tf_op jit(solution)/shard_map/reduce_scatter | solution.py:85
Sparse Core Ops, SparseCore 0:
  41.6 50.7 all-reduce.1
  96.0 30.9 reduce-scatter.1
where the time goes:
time: 136 us; the launch traced here: 135 us
  waiting for transfers between devices  100 us (74%)
  between operations  14.2 us (10%)
  other arithmetic  8.38 us (6%)
  starting transfers between devices  6.27 us (5%)
  local copies, waits for them, and re-layouts  4.45 us (3%)
  matrix products  1.77 us (1%)
    psum x1, waiting for transfers between devices, per_device(): summed = lax.psum(traces, 'tm')  50.9 us
    reduce_scatter x1, waiting for transfers between devices, per_device(): lax.psum_scatter(jnp.einsum('rt,tpl->rpl', membership, own_rows, precisio...  31.1 us
    ppermute x8, waiting for transfers between devices, shifted(): return lax.ppermute(block, axis, route)  18.1 us
    ppermute x8, starting transfers between devices, shifted(): return lax.ppermute(block, axis, route)  6.23 us
    cos x1, other arithmetic, phase_tables(): return (jnp.cos(angle), jnp.sin(angle))  4.29 us
  transfers between devices with their start and end apart: 10, of which 10 were waited for; matrix products, arithmetic and copies ran while one was open for 0% of the time, Pallas kernels for 0%

commit v1 on v0

--- a/solution.py
+++ b/solution.py
@@ -10,6 +10,15 @@
 GROUP = 64
 SRC = 4
 PAIRS = 128
+
+
+def sum_by_hops(x, axis):
+    devices = lax.axis_size(axis)
+    total, far = (x, 1)
+    while far < devices:
+        total = total + lax.ppermute(total, axis, [(i, i ^ far) for i in range(devices)])
+        far = 2 * far
+    return total
 
 
 def shifted(block, axis, distance):
@@ -78,7 +87,7 @@
     modulated = modulate(source_rows, cosines, sines)
     correlation = jnp.einsum("ck,ikl->icl", whitened, modulated, preferred_element_type=jnp.float32)
     traces = normalize(correlation)
-    summed = lax.psum(traces, "tm")
+    summed = sum_by_hops(traces, "tm")
     row_count = PAIRS // lax.axis_size("tm")
     own_rows = lax.dynamic_slice_in_dim(summed, lax.axis_index("tm") * row_count, row_count, 1)
     membership = (owner_bins[:, None] == tile_bin[None, :]).astype(jnp.float32)

time: 136 us -> 125 us (0.919)
  waiting for transfers between devices: 100 us -> 88.7 us
  starting transfers between devices: 6.27 us -> 9.37 us
  local copies, waits for them, and re-layouts: 4.45 us -> 2.57 us
    psum x1 -> x0, waiting for transfers between devices: 50.9 us -> none  [per_device(): summed = lax.psum(traces, 'tm')]
    ppermute x0 -> x2, waiting for transfers between devices: none -> 39.7 us  [sum_by_hops(): lax.ppermute(total, axis, [(i, i ^ far) for i in range(devices)])]
    ppermute x0 -> x2, starting transfers between devices: none -> 3.14 us  [sum_by_hops(): lax.ppermute(total, axis, [(i, i ^ far) for i in range(devices)])]
    dynamic_slice x2 -> x0, local copies, waits for them, and re-layouts: 1.89 us -> none  [per_device(): lax.dynamic_slice_in_dim(summed, lax.axis_index('tm') * row_count, row_co...]
  transfers between devices with their start and end apart: 10 -> 11, of which waited for: 10 -> 11; matrix products, arithmetic and copies ran while one was open for 0% -> 0% of each run, Pallas kernels for 0% -> 0%
where the time goes in v1:
time: 125 us; the launch traced here: 124 us
  waiting for transfers between devices  88.7 us (71%)
  between operations  14.3 us (11%)
  starting transfers between devices  9.37 us (7%)
  other arithmetic  7.69 us (6%)
  local copies, waits for them, and re-layouts  2.57 us (2%)
  matrix products  1.78 us (1%)
    ppermute x2, waiting for transfers between devices, sum_by_hops(): lax.ppermute(total, axis, [(i, i ^ far) for i in range(devices)])  39.7 us
    reduce_scatter x1, waiting for transfers between devices, per_device(): lax.psum_scatter(jnp.einsum('rt,tpl->rpl', membership, own_rows, precisio...  30.9 us
    ppermute x8, waiting for transfers between devices, shifted(): return lax.ppermute(block, axis, route)  18.1 us
    ppermute x8, starting transfers between devices, shifted(): return lax.ppermute(block, axis, route)  6.23 us
    cos x1, other arithmetic, phase_tables(): return (jnp.cos(angle), jnp.sin(angle))  4.28 us
    ppermute x2, starting transfers between devices, sum_by_hops(): lax.ppermute(total, axis, [(i, i ^ far) for i in range(devices)])  3.14 us
  transfers between devices with their start and end apart: 11, of which 11 were waited for; matrix products, arithmetic and copies ran while one was open for 0% of the time, Pallas kernels for 0%

profile of v1, /device:TPU:0, one launch (start us, length us, event | category | flops | bytes accessed | tf_op | source)
XLA Modules:
  0.0 124.4 jit_solution(9700316065813235927)
XLA Ops:
  6.5 0.0 reduce-scatter.2.cloned.1.call-start
  7.3 1.1 copy.14
  8.5 0.1 fusion.11
  8.6 0.1 broadcast_select_fusion
  8.7 0.1 copy.17
  8.9 0.1 copy.15
  9.0 24.5 %while.19 = (s32[]{:T(128)}, bf16[4,1024]{1,0:T(4,128)(2,1)S(1)}, bf16[4,1024]{1,0:T(4,128)(2,1)S(1)}, bf16[4,1024]{1,0:T(4,128)(2,1)S(1)}, s32[]{:T(128)}, /*in...) while((s32[]{:T(128)}, bf16[4,1024]{1,0:T(4,128)(2,1)S(1)}, bf16[4,1024]{1,0:T(4,128)(2,1)S(1)}, ...), condition=%wide.region_2.3_spmd, body=%wide.region_1.2_spmd.sunk | while | flops 8220 | bytes 131515 | solution.py:83
  9.0 4.5 %collective-permute-start.1 = (bf16[4,1024]{1,0:T(4,128)(2,1)S(1)}, bf16[4,1024]{1,0:T(4,128)(2,1)S(1)}, u32[]{:S(2)}, u32[]{:S(2)}) collective-permute-start(bf16[4,1024]{1,0:T(4,128)(2,1)S(1)} %get-tuple-element.246), channel_id=1, source_target_pairs={{4,0},{8,4},{12,8},{16,12},{20,16},{24,20},{28,24},{0,28},{5,1},{9... | collective-permute-start | bytes 24584 | tf_op jit(solution)/shard_map/while/body/eval_jaxpr/ppermute | solution.py:27
  13.6 0.0 collective-permute-start
  13.6 1.4 %collective-permute-done.1 = bf16[4,1024]{1,0:T(4,128)(2,1)S(1)} collective-permute-done((bf16[4,1024]{1,0:T(4,128)(2,1)S(1)}, bf16[4,1024]{1,0:T(4,128)(2,1)S(1)}, u32[]{:S(2)}, u32[]{:S(2)}) %collective-permute-start.1) | collective-permute-done | bytes 8224 | tf_op jit(solution)/shard_map/while/body/eval_jaxpr/ppermute | solution.py:27
  15.0 3.5 %collective-permute-done = bf16[4,1024]{1,0:T(4,128)(2,1)S(1)} collective-permute-done((bf16[4,1024]{1,0:T(4,128)(2,1)S(1)}, bf16[4,1024]{1,0:T(4,128)(2,1)S(1)}, u32[]{:S(2)}, u32[]{:S(2)}) %collective-permute-start) | collective-permute-done | bytes 8224 | tf_op jit(solution)/shard_map/while/body/eval_jaxpr/ppermute | solution.py:27
  18.5 0.1 collective-permute-start.1
  18.6 0.5 collective-permute-start
  19.1 0.9 collective-permute-done.1
  19.9 3.5 %collective-permute-done = bf16[4,1024]{1,0:T(4,128)(2,1)S(1)} collective-permute-done((bf16[4,1024]{1,0:T(4,128)(2,1)S(1)}, bf16[4,1024]{1,0:T(4,128)(2,1)S(1)}, u32[]{:S(2)}, u32[]{:S(2)}) %collective-permute-start) | collective-permute-done | bytes 8224 | tf_op jit(solution)/shard_map/while/body/eval_jaxpr/ppermute | solution.py:27
  23.5 0.1 collective-permute-start.1
  23.6 0.4 collective-permute-start
  24.1 0.9 collective-permute-done.1
  25.0 3.5 %collective-permute-done = bf16[4,1024]{1,0:T(4,128)(2,1)S(1)} collective-permute-done((bf16[4,1024]{1,0:T(4,128)(2,1)S(1)}, bf16[4,1024]{1,0:T(4,128)(2,1)S(1)}, u32[]{:S(2)}, u32[]{:S(2)}) %collective-permute-start) | collective-permute-done | bytes 8224 | tf_op jit(solution)/shard_map/while/body/eval_jaxpr/ppermute | solution.py:27
  28.5 0.1 collective-permute-start.1
  28.6 0.5 collective-permute-start
  29.1 0.9 collective-permute-done.1
  30.0 3.5 %collective-permute-done = bf16[4,1024]{1,0:T(4,128)(2,1)S(1)} collective-permute-done((bf16[4,1024]{1,0:T(4,128)(2,1)S(1)}, bf16[4,1024]{1,0:T(4,128)(2,1)S(1)}, u32[]{:S(2)}, u32[]{:S(2)}) %collective-permute-start) | collective-permute-done | bytes 8224 | tf_op jit(solution)/shard_map/while/body/eval_jaxpr/ppermute | solution.py:27
  33.6 4.3 %fusion.9 = (f32[512,512]{1,0:T(8,128)S(1)}, f32[512,512]{1,0:T(8,128)S(1)}) fusion(s32[512]{0:T(512)S(1)} %get-tuple-element.195, s32[512]{0:T(512)S(1)} %get-tuple-element.196), kind=kLoop, calls=%fused_computation.16 | loop fusion | flops 2359296 | bytes 2101248 | tf_op jit(solution)/shard_map/cos | solution.py:45
  37.9 1.2 add_convert_fusion
  39.1 1.2 multiply_reduce_fusion
  40.3 0.1 divide_bitcast_fusion
  40.4 0.0 copy-start
  40.4 0.0 copy-start.1
  40.4 1.6 %collective-permute-start.2 = (f32[4,128,512]{2,1,0:T(8,128)S(1)}, f32[4,128,512]{2,1,0:T(8,128)S(1)}, u32[]{:S(2)}, u32[]{:S(2)}) collective-permute-start(f32[4,128,512]{2,1,0:T(8,128)S(1)} %divide_bitcast_fusion), channel_id=1, source_target_pairs={{0,1},{1,0},{2,3},{3,2},{4,5},{5,4},{6,7},{7,6},{8,9},{9,8},{10,11... | collective-permute-start | bytes 3145736 | tf_op jit(solution)/shard_map/ppermute | solution.py:19
  42.0 20.3 %collective-permute-done.2 = f32[4,128,512]{2,1,0:T(8,128)S(1)} collective-permute-done((f32[4,128,512]{2,1,0:T(8,128)S(1)}, f32[4,128,512]{2,1,0:T(8,128)S(1)}, u32[]{:S(2)}, u32[]{:S(2)}) %collective-permute-start.2) | collective-permute-done | bytes 1048608 | tf_op jit(solution)/shard_map/ppermute | solution.py:19
  62.3 0.2 fusion.23
  62.5 1.6 %collective-permute-start.3 = (f32[4,128,512]{2,1,0:T(8,128)S(1)}, f32[4,128,512]{2,1,0:T(8,128)S(1)}, u32[]{:S(2)}, u32[]{:S(2)}) collective-permute-start(f32[4,128,512]{2,1,0:T(8,128)S(1)} %fusion.23), channel_id=1, source_target_pairs={{0,2},{1,3},{2,0},{3,1},{4,6},{5,7},{6,4},{7,5},{8,10},{9,11},{10,... | collective-permute-start | bytes 3145736 | tf_op jit(solution)/shard_map/ppermute | solution.py:19
  64.1 19.4 %collective-permute-done.3 = f32[4,128,512]{2,1,0:T(8,128)S(1)} collective-permute-done((f32[4,128,512]{2,1,0:T(8,128)S(1)}, f32[4,128,512]{2,1,0:T(8,128)S(1)}, u32[]{:S(2)}, u32[]{:S(2)}) %collective-permute-start.3) | collective-permute-done | bytes 1048608 | tf_op jit(solution)/shard_map/ppermute | solution.py:19
  83.5 0.0 copy-done
  83.5 0.0 copy-done.1
  83.5 0.6 fusion.15
  84.1 1.1 copy.20
  85.2 0.0 reduce-scatter.2.cloned.1.call-update
  85.3 30.9 %reduce-scatter.2.cloned.1.call-done = f32[1,32,512]{2,1,0:T(8,128)} async-done(((f32[8,32,512]{2,1,0:T(8,128)}), f32[1,32,512]{2,1,0:T(8,128)}) %reduce-scatter.2.cloned.1.call-update) | async-done | bytes 65552 | tf_op jit(solution)/shard_map/reduce_scatter | solution.py:94
  116.1 1.5 %broadcast_multiply_fusion = f32[1,32,512]{2,1,0:T(8,128)} fusion(f32[1,32,512]{2,1,0:T(8,128)} %reduce-scatter.2.cloned.1.call-done), kind=kLoop, calls=%fused_computation.29 | loop fusion | flops 16384 | bytes 131072 | tf_op jit(solution)/shard_map/div | solution.py:100
  (20 shorter events, 0.3 us)
Async XLA Ops:
  6.5 109.6 %reduce-scatter.2.cloned.1.call-start = ((), (), s32[]{:S(2)}) async-start(), calls=%async_computation.1 | async-start | bytes 589824 | tf_op jit(solution)/shard_map/reduce_scatter | solution.py:94
  9.0 5.9 %collective-permute-start.1 = (bf16[4,1024]{1,0:T(4,128)(2,1)S(1)}, bf16[4,1024]{1,0:T(4,128)(2,1)S(1)}, u32[]{:S(2)}, u32[]{:S(2)}) collective-permute-start(bf16[4,1024]{1,0:T(4,128)(2,1)S(1)} %get-tuple-element.246), channel_id=1, source_target_pairs={{4,0},{8,4},{12,8},{16,12},{20,16},{24,20},{28,24},{0,28},{5,1},{9... | collective-permute-start | bytes 24584 | tf_op jit(solution)/shard_map/while/body/eval_jaxpr/ppermute | solution.py:27
  13.6 4.9 %collective-permute-start = (bf16[4,1024]{1,0:T(4,128)(2,1)S(1)}, bf16[4,1024]{1,0:T(4,128)(2,1)S(1)}, u32[]{:S(2)}, u32[]{:S(2)}) collective-permute-start(bf16[4,1024]{1,0:T(4,128)(2,1)S(1)} %get-tuple-element.245), channel_id=1, source_target_pairs={{28,0},{0,4},{4,8},{8,12},{12,16},{16,20},{20,24},{24,28},{29,1},{... | collective-permute-start | bytes 24584 | tf_op jit(solution)/shard_map/while/body/eval_jaxpr/ppermute | solution.py:27
  18.5 1.4 %collective-permute-start.1 = (bf16[4,1024]{1,0:T(4,128)(2,1)S(1)}, bf16[4,1024]{1,0:T(4,128)(2,1)S(1)}, u32[]{:S(2)}, u32[]{:S(2)}) collective-permute-start(bf16[4,1024]{1,0:T(4,128)(2,1)S(1)} %get-tuple-element.246), channel_id=1, source_target_pairs={{4,0},{8,4},{12,8},{16,12},{20,16},{24,20},{28,24},{0,28},{5,1},{9... | collective-permute-start | bytes 24584 | tf_op jit(solution)/shard_map/while/body/eval_jaxpr/ppermute | solution.py:27
  18.6 4.9 %collective-permute-start = (bf16[4,1024]{1,0:T(4,128)(2,1)S(1)}, bf16[4,1024]{1,0:T(4,128)(2,1)S(1)}, u32[]{:S(2)}, u32[]{:S(2)}) collective-permute-start(bf16[4,1024]{1,0:T(4,128)(2,1)S(1)} %get-tuple-element.245), channel_id=1, source_target_pairs={{28,0},{0,4},{4,8},{8,12},{12,16},{16,20},{20,24},{24,28},{29,1},{... | collective-permute-start | bytes 24584 | tf_op jit(solution)/shard_map/while/body/eval_jaxpr/ppermute | solution.py:27
  23.5 1.5 %collective-permute-start.1 = (bf16[4,1024]{1,0:T(4,128)(2,1)S(1)}, bf16[4,1024]{1,0:T(4,128)(2,1)S(1)}, u32[]{:S(2)}, u32[]{:S(2)}) collective-permute-start(bf16[4,1024]{1,0:T(4,128)(2,1)S(1)} %get-tuple-element.246), channel_id=1, source_target_pairs={{4,0},{8,4},{12,8},{16,12},{20,16},{24,20},{28,24},{0,28},{5,1},{9... | collective-permute-start | bytes 24584 | tf_op jit(solution)/shard_map/while/body/eval_jaxpr/ppermute | solution.py:27
  23.6 4.9 %collective-permute-start = (bf16[4,1024]{1,0:T(4,128)(2,1)S(1)}, bf16[4,1024]{1,0:T(4,128)(2,1)S(1)}, u32[]{:S(2)}, u32[]{:S(2)}) collective-permute-start(bf16[4,1024]{1,0:T(4,128)(2,1)S(1)} %get-tuple-element.245), channel_id=1, source_target_pairs={{28,0},{0,4},{4,8},{8,12},{12,16},{16,20},{20,24},{24,28},{29,1},{... | collective-permute-start | bytes 24584 | tf_op jit(solution)/shard_map/while/body/eval_jaxpr/ppermute | solution.py:27
  28.5 1.4 %collective-permute-start.1 = (bf16[4,1024]{1,0:T(4,128)(2,1)S(1)}, bf16[4,1024]{1,0:T(4,128)(2,1)S(1)}, u32[]{:S(2)}, u32[]{:S(2)}) collective-permute-start(bf16[4,1024]{1,0:T(4,128)(2,1)S(1)} %get-tuple-element.246), channel_id=1, source_target_pairs={{4,0},{8,4},{12,8},{16,12},{20,16},{24,20},{28,24},{0,28},{5,1},{9... | collective-permute-start | bytes 24584 | tf_op jit(solution)/shard_map/while/body/eval_jaxpr/ppermute | solution.py:27
  28.6 4.9 %collective-permute-start = (bf16[4,1024]{1,0:T(4,128)(2,1)S(1)}, bf16[4,1024]{1,0:T(4,128)(2,1)S(1)}, u32[]{:S(2)}, u32[]{:S(2)}) collective-permute-start(bf16[4,1024]{1,0:T(4,128)(2,1)S(1)} %get-tuple-element.245), channel_id=1, source_target_pairs={{28,0},{0,4},{4,8},{8,12},{12,16},{16,20},{20,24},{24,28},{29,1},{... | collective-permute-start | bytes 24584 | tf_op jit(solution)/shard_map/while/body/eval_jaxpr/ppermute | solution.py:27
  40.4 43.1 %copy-start = (s32[8]{0:T(128)S(1)}, s32[8]{0:T(128)}, u32[]{:S(2)}) copy-start(s32[8]{0:T(128)} %param.8) | copy-start | bytes 100
  40.4 43.1 %copy-start.1 = (s32[4]{0:T(128)S(1)}, s32[4]{0:T(128)}, u32[]{:S(2)}) copy-start(s32[4]{0:T(128)} %param.7) | copy-start | bytes 52
  40.4 21.9 %collective-permute-start.2 = (f32[4,128,512]{2,1,0:T(8,128)S(1)}, f32[4,128,512]{2,1,0:T(8,128)S(1)}, u32[]{:S(2)}, u32[]{:S(2)}) collective-permute-start(f32[4,128,512]{2,1,0:T(8,128)S(1)} %divide_bitcast_fusion), channel_id=1, source_target_pairs={{0,1},{1,0},{2,3},{3,2},{4,5},{5,4},{6,7},{7,6},{8,9},{9,8},{10,11... | collective-permute-start | bytes 3145736 | tf_op jit(solution)/shard_map/ppermute | solution.py:19
  62.5 20.9 %collective-permute-start.3 = (f32[4,128,512]{2,1,0:T(8,128)S(1)}, f32[4,128,512]{2,1,0:T(8,128)S(1)}, u32[]{:S(2)}, u32[]{:S(2)}) collective-permute-start(f32[4,128,512]{2,1,0:T(8,128)S(1)} %fusion.23), channel_id=1, source_target_pairs={{0,2},{1,3},{2,0},{3,1},{4,6},{5,7},{6,4},{7,5},{8,10},{9,11},{10,... | collective-permute-start | bytes 3145736 | tf_op jit(solution)/shard_map/ppermute | solution.py:19
Sparse Core Ops, SparseCore 0:
  85.4 30.6 reduce-scatter.1
